TPU v7x, 32 devices: a whole 2x2x4 slice. The times are simulated.
32 devices in a mesh: groups: 2 (over x), tm: 16 (over z, y, core).
Axes of the slice: x: 2, y: 2, z: 4, core: 2. Of those that a mesh axis runs over, the one named last changes fastest.
Arguments:
- states: bfloat16 [4096, 2, 1024], P('tm', 'groups'), parts along dimension 1, may hold values from -6 to 6
- goals: bfloat16 [4096, 2, 1024], P('tm', 'groups'), parts along dimension 1, may hold values from -6 to 6
- pos_offset: int32 [16, 2, 8], P('tm', 'groups'), parts along dimension 1, may hold values from 0 to 15
- neg_blocks: int32 [16, 2, 16], P('tm', 'groups'), parts along dimension 1, may hold values from 0 to 15
Outputs:
- loss_mean: float32 [2], P('groups'), parts along dimension 0
- grad_states: float32 [4096, 2, 1024], P('tm', 'groups'), parts along dimension 1
- grad_goals: float32 [4096, 2, 1024], P('tm', 'groups'), parts along dimension 1
There are 2 independent parts, one for each index of `groups`. A program takes and returns all parts, laid end to end along the dimension named above; each array names one. Nothing has to cross between parts.
All inputs are finite; a program needn't handle non-finite values.
Results may differ from a plain program's by a relative error of at most 0.012.
Values may be sent and summed in bfloat16 or wider, within the bound.
No kernel may reach another device: no remote copies, remote signals or barrier semaphores. Data moves between devices by JAX's collectives and lax.ppermute only.
A program may use at most 128 MiB of HBM per device.

v0:
```python
import functools
import math

import jax
import jax.numpy as jnp
from jax import lax
from jax.experimental import pallas as pl
from jax.experimental.pallas import tpu as pltpu
from jax.sharding import PartitionSpec as P


AXIS = "tm"


def swap(value, offset, size, only=lambda i: True):
    return lax.ppermute(value, AXIS, [(i, i ^ offset) for i in range(size) if only(i)])


def subsets(bits):
    found = [0]
    for bit in bits:
        found = found + [offset ^ bit for offset in found]
    return found


def fold(part, op):
    pieces = [part[k : k + 8] for k in range(0, part.shape[0], 8)]
    while len(pieces) > 1:
        pieces = [op(*pieces[k : k + 2]) if k + 1 < len(pieces) else pieces[k] for k in range(0, len(pieces), 2)]
    return pieces[0]


def tile_kernel(plan, own_ref, *refs):
    n_new = len(plan["row_places"]) + len(plan["col_places"])
    tables, refs = refs[: plan["n_tables"]], refs[plan["n_tables"] :]
    arrived, refs = refs[:n_new], refs[n_new:]
    if plan["aliased"] or not plan["new"]:
        held, refs = refs[:3], refs[3:]
    if plan["new"]:
        loss_ref, held, refs = refs[0], refs[1:4], refs[4:]
    rows, cols, coeff = held
    row_out, refs = refs[: len(plan["row_outs"])], refs[len(plan["row_outs"]) :]
    col_out, (fresh, sem) = refs[: len(plan["col_outs"])], refs[len(plan["col_outs"]) :]
    width = rows.shape[1]
    inv_root = 1.0 / math.sqrt(width)
    size = tables[0].shape[0] // 2 if tables else 0

    targets = [rows.at[pl.ds(p, r.shape[0])] for p, r in zip(plan["row_places"], arrived)]
    targets += [cols.at[pl.ds(p, r.shape[0])] for p, r in zip(plan["col_places"], arrived[len(targets) :])]
    loads = [pltpu.make_async_copy(s, t, sem.at[k]) for k, (s, t) in enumerate(zip(arrived, targets))]
    for copy in loads:
        copy.start()
    for copy in loads:
        copy.wait()

    if plan["new"]:
        own = own_ref[0]
        loss = jnp.zeros((8, 128), jnp.float32)
        at, kept = 0, []
        for r0, r1, c0, c1 in plan["new"]:
            buffer = fresh.at[pl.ds(at, c1 - c0), pl.ds(0, r1 - r0)]
            at += c1 - c0
            kept.append((buffer, coeff.at[pl.ds(c0, c1 - c0), pl.ds(r0, r1 - r0)]))
            dots = lax.dot_general(
                cols[c0:c1, :], rows[r0:r1, :], (((1,), (1,)), ((), ())), preferred_element_type=jnp.float32
            )
            for cp, cl, j, c_off in plan["col_chunks"]:
                if cp < c0 or cp >= c1:
                    continue
                target = own ^ plan["col_xors"][j]
                for rp, rl, i, r_off in plan["row_chunks"]:
                    if rp < r0 or rp >= r1:
                        continue
                    raw = dots[cp - c0 : cp - c0 + cl, rp - r0 : rp - r0 + rl]
                    pos, neg = tables[i][target], tables[i][size + target]
                    decay = jnp.exp2(jnp.abs(raw) * (-inv_root * math.log2(math.e)))
                    whole = 1.0 + decay
                    large = pl.reciprocal(whole)
                    up = raw >= 0.0
                    above = jnp.maximum(raw, 0.0)
                    if plan["row_xors"][i] == plan["col_xors"][j]:
                        later = lax.broadcasted_iota(jnp.int32, raw.shape, 0) + c_off > (
                            lax.broadcasted_iota(jnp.int32, raw.shape, 1) + r_off
                        )
                        pos = jnp.where(later, pos, 0.0)
                        soft = jnp.log(whole)
                        above, below = above * inv_root, (above - raw) * inv_root
                        part = fold(pos * (below + soft) + neg * (above + soft), jnp.add)
                    else:
                        over, total = fold(above, jnp.add) * inv_root, fold(raw, jnp.add) * inv_root
                        part = neg * over + pos * (over - total)
                        part = part + (pos + neg) * jnp.log(fold(whole, jnp.multiply))
                    gain, drop = neg * inv_root, pos * inv_root
                    values = (jnp.where(up, gain, -drop) + jnp.where(up, -drop, gain) * decay) * large
                    for k in range(0, part.shape[1], 128):
                        loss = loss + part[:, k : k + 128]
                    buffer[cp - c0 : cp - c0 + cl, rp - r0 : rp - r0 + rl] = values.astype(jnp.bfloat16)
        loss_ref[...] = loss
        copies = [pltpu.make_async_copy(s, t, sem.at[n_new + k]) for k, (s, t) in enumerate(kept)]
        for copy in copies:
            copy.start()
        for copy in copies:
            copy.wait()

    def finish(outs, pieces, compute):
        if not outs:
            return
        low, high = min(p[0] for out in pieces for p in out), max(p[1] for out in pieces for p in out)
        for base in range(low, high, plan["step"]):
            top = min(high, base + plan["step"])
            value = compute(base, top)
            for out, parts in zip(outs, pieces):
                at = 0
                for p0, p1 in parts:
                    a, b = max(p0, base), min(p1, top)
                    if a < b:
                        out[at + a - p0 : at + b - p0, :] = value[a - base : b - base].astype(out.dtype)
                    at += p1 - p0

    finish(row_out, plan["row_outs"], lambda a, b: lax.dot_general(
        coeff[:, a:b], cols[...], (((0,), (0,)), ((), ())), preferred_element_type=jnp.float32))
    finish(col_out, plan["col_outs"], lambda a, b: jnp.dot(
        coeff[a:b, :], rows[...], preferred_element_type=jnp.float32))


def phase(own, tables, rows, cols, held, row_chunks, col_chunks, row_xors, col_xors, new=(), row_outs=(),
          col_outs=(), dtypes=None):
    n_row, n_col = (sum(c[1] for c in chunks) for chunks in (row_chunks, col_chunks))
    tables = tables if new else []
    width = next(iter(rows.values())).shape[1] if rows else held[0].shape[1]
    plan = dict(
        row_chunks=row_chunks, col_chunks=col_chunks, row_xors=row_xors, col_xors=col_xors, n_tables=len(tables),
        row_places=list(rows), col_places=list(cols), aliased=held is not None, new=new, row_outs=row_outs,
        col_outs=col_outs, step=512,
    )
    smem, anywhere, vmem = (pl.BlockSpec(memory_space=m) for m in (pltpu.SMEM, pl.ANY, pltpu.VMEM))
    args = [own, *tables, *rows.values(), *cols.values()]
    in_specs = [smem] * (1 + len(tables)) + [anywhere] * (len(rows) + len(cols))
    out_shape, aliases = [], {}
    if new:
        out_shape.append(pltpu.VMEM((8, 128), jnp.float32))
        if held is not None:
            aliases = {len(args) + k: 1 + k for k in range(3)}
        out_shape += [
            pltpu.VMEM(shape, jnp.bfloat16) for shape in ((n_row, width), (n_col, width), (n_col, n_row))
        ]
    if held is not None:
        args += [pltpu.with_memory_space_constraint(x, pltpu.VMEM) for x in held]
        in_specs += [vmem] * 3
    outs = (*row_outs, *col_outs)
    lengths = [sum(b - a for a, b in out) for out in outs]
    dtypes = dtypes or [jnp.bfloat16] * len(lengths)
    out_shape += [pltpu.VMEM((n, width), dtype) for n, dtype in zip(lengths, dtypes)]
    row_total, col_total = sum(lengths[: len(row_outs)]), sum(lengths[len(row_outs) :])
    area = sum((r1 - r0) * (c1 - c0) for r0, r1, c0, c1 in new)
    flops = 2 * width * (area + row_total * n_col + col_total * n_row)
    outs = list(
        pl.pallas_call(
            functools.partial(tile_kernel, plan),
            in_specs=in_specs,
            out_specs=[vmem] * len(out_shape),
            out_shape=out_shape,
            input_output_aliases=aliases,
            scratch_shapes=[
                pltpu.VMEM(
                    (max(16, sum(c1 - c0 for _, _, c0, c1 in new)), max([128] + [r1 - r0 for r0, r1, _, _ in new])),
                    jnp.bfloat16,
                ),
                pltpu.SemaphoreType.DMA((max(1, len(rows) + len(cols) + len(new)),)),
            ],
            cost_estimate=pl.CostEstimate(flops=flops, bytes_accessed=4 * width * width, transcendentals=2 * area),
            compiler_params=pltpu.CompilerParams(vmem_limit_bytes=20 << 20),
        )(*args)
    )
    loss = outs.pop(0) if new else None
    if new:
        held, outs = outs[:3], outs[3:]
    return loss, held, outs[: len(row_outs)], outs[len(row_outs) :]


def counts(pos_offset, neg_blocks, size):
    blocks = jnp.arange(size, dtype=jnp.int32)
    target = lax.axis_index(AXIS).astype(jnp.int32) + pos_offset.reshape(-1)
    pos = jnp.sum((target[:, None] == blocks).astype(jnp.float32), axis=0)
    neg = jnp.sum((neg_blocks.reshape(-1)[:, None] == blocks).astype(jnp.float32), axis=0)
    return jnp.concatenate([pos, neg])


def add_kernel(starts, *refs):
    *parts, out = refs
    out[...] = sum(
        part[start : start + out.shape[0], :].astype(jnp.float32) for start, part in zip(starts, parts)
    ).astype(out.dtype)


def add(rows, *parts):
    vmem = pl.BlockSpec(memory_space=pltpu.VMEM)
    width = parts[0][0].shape[1]
    return pl.pallas_call(
        functools.partial(add_kernel, [start for _, start in parts]),
        in_specs=[vmem] * len(parts),
        out_specs=vmem,
        out_shape=pltpu.VMEM((rows, width), jnp.bfloat16),
        cost_estimate=pl.CostEstimate(
            flops=rows * width * len(parts), bytes_accessed=4 * rows * width, transcendentals=0
        ),
        compiler_params=pltpu.CompilerParams(vmem_limit_bytes=4 << 20),
    )(*[pltpu.with_memory_space_constraint(part, pltpu.VMEM) for part, _ in parts])


def finish_kernel(n_loss, firsts, in_place, count, start, *refs):
    n_part = len(firsts)
    losses, parts, refs = refs[:n_loss], refs[n_loss : n_loss + n_part], refs[n_loss + n_part + in_place :]
    *outs, total, sem = refs
    if n_loss:
        outs[-2][0] = jnp.sum(sum(loss[...] for loss in losses)) * (1.0 / count)
    rows, n, stores = total.shape[0], 64, []
    for r in range(0, rows, n):
        here = pl.ds(r, n)
        total[here, :] = sum(part[f + r : f + r + n, :].astype(jnp.float32) for f, part in zip(firsts, parts))
        there = outs[-1].at[pl.ds(start + r, n), 0, :]
        stores.append(pltpu.make_async_copy(total.at[here], there, sem.at[len(stores)]))
        stores[-1].start()
    for copy in stores:
        copy.wait()


def finish_rows(rows, parts, length, start=0, into=None, losses=(), count=1):
    width = parts[0][0].shape[1]
    smem, anywhere, vmem = (pl.BlockSpec(memory_space=m) for m in (pltpu.SMEM, pl.ANY, pltpu.VMEM))
    held = [pltpu.with_memory_space_constraint(x, pltpu.VMEM) for x in (*losses, *(block for block, _ in parts))]
    out_shape = [jax.ShapeDtypeStruct((length, 1, width), jnp.float32)]
    out_specs = [anywhere]
    if losses:
        out_shape, out_specs = [jax.ShapeDtypeStruct((1,), jnp.float32), *out_shape], [smem, anywhere]
    in_place = into is not None
    return pl.pallas_call(
        functools.partial(finish_kernel, len(losses), [first for _, first in parts], in_place, count, start),
        in_specs=[vmem] * len(held) + [anywhere] * in_place,
        out_specs=out_specs,
        out_shape=out_shape,
        input_output_aliases={len(held): len(out_shape) - 1} if in_place else {},
        scratch_shapes=[pltpu.VMEM((rows, width), jnp.float32), pltpu.SemaphoreType.DMA((rows // 64,))],
        cost_estimate=pl.CostEstimate(flops=4 * rows * width, bytes_accessed=14 * rows * width, transcendentals=0),
        compiler_params=pltpu.CompilerParams(vmem_limit_bytes=8 << 20),
    )(*held, *([into] if in_place else []))


def step(states, goals, pos_offset, neg_blocks):
    size = lax.axis_size(AXIS)
    length, width = states.shape[0], states.shape[2]
    half = length // 2
    high = size // 2
    inner = []
    bit = size // 4
    while bit > 1:
        inner.append(bit)
        bit //= 2
    across = high ^ (high >> 1)
    blocks = subsets(inner)
    n_block = len(blocks)
    row_xors, col_xors = [0, across], [x ^ side for x in blocks for side in (0, 1)]
    n_row, n_col = len(row_xors) * length, len(col_xors) * length
    last = n_col - 2 * length
    state, goal = states.reshape(length, width), goals.reshape(length, width)
    own = lax.axis_index(AXIS).astype(jnp.int32).reshape(1)

    def outer(i):
        return (i & across) in (0, across)

    mine = [goal]
    for bit in inner:
        mine = mine + [swap(block, bit, size) for block in mine]
    side = [swap(block, 1, size) for block in mine]
    cols = {2 * k * length + p: b for k in range(n_block) for p, b in ((0, mine[k]), (length, side[k]))}
    pair_in = swap(state, across, size, lambda i: not outer(i))
    pair = pair_in + swap(state, across, size, outer)
    table = counts(pos_offset, neg_blocks, size)
    tables = [table, swap(table, across, size)]

    fixed = dict(
        row_xors=row_xors, col_xors=col_xors,
        row_chunks=tuple((k * length, length, k, 0) for k in range(len(row_xors))),
        col_chunks=tuple((k * length, length, k, 0) for k in range(len(col_xors))),
    )

    def arrived(start, end):
        return {p: c for p, c in cols.items() if start <= p < end}

    loss_a, held, _, _ = phase(
        own, tables[:1], {0: state}, arrived(0, length), None, new=[(0, length, 0, length)], **fixed
    )
    loss_b, held, _, _ = phase(
        own, tables[:1], {}, arrived(length, last), held, new=[(0, length, length, last)], **fixed
    )
    loss_c, held, _, _ = phase(own, tables, {length: pair}, {}, held, new=[(length, n_row, 0, last)], **fixed)
    sides, own_sums = {}, {}

    def goal_phase(which, tables, cols, held, new, rows=()):
        pieces = [[(p * length, (p + 1) * length)] for k in which for p in (2 * k + 1, 2 * k)]
        loss, held, row_outs, outs = phase(
            own, tables, {}, cols, held, new=new, row_outs=rows, col_outs=pieces,
            dtypes=[jnp.float32] * len(rows) + [jnp.bfloat16, jnp.float32] * len(which), **fixed,
        )
        sides.update(zip(which, outs[0::2]))
        own_sums.update(zip(which, outs[1::2]))
        return loss, held, row_outs

    top = n_block // 2
    loss_d, held, _ = goal_phase(
        list(range(n_block - 1, top, -1)), tables, arrived(last, n_col), held, [(0, n_row, last, n_col)]
    )
    loss = loss_a + loss_b + loss_c + loss_d
    _, _, (pair_part,), _ = phase(own, [], {}, {}, held, row_outs=[[(length, n_row)]], **fixed)

    back_pair = swap(pair_part, across, size)
    goal_phase([top], [], {}, held, ())
    _, _, (own_part,) = goal_phase(list(range(top)), [], {}, held, (), rows=[[(0, length)]])
    cross = {k: swap(part, 1, size) for k, part in sides.items()}
    loss = loss + swap(loss, 1, size)
    for s in reversed(range(len(inner))):
        loss = loss + swap(loss, inner[s], size)
    losses = [loss, swap(loss, across, size)]
    addends = {k: [(own_sums[k], 0), (cross[k], 0)] for k in range(n_block)}
    halves = {(k, o): [] for k in range(n_block) for o in (0, half)}
    for s in reversed(range(len(inner))):
        for k in reversed(range(1 << s, 2 << s)):
            to = k - (1 << s)
            for o in (0, half):
                piece = add(half, *[(b, o) for b, _ in addends[k]], *[(b, 0) for b in halves[k, o]])
                halves[to, o].append(swap(piece, inner[s], size))
    pieces = [[(block, o) for block, _ in addends[0]] + [(block, 0) for block in halves[0, o]] for o in (0, half)]
    (grad_goals,) = finish_rows(half, pieces[0], length)
    loss_mean, grad_states = finish_rows(
        length, [(own_part, 0), (back_pair, 0)], length, losses=losses, count=size * length
    )
    (grad_goals,) = finish_rows(half, pieces[1], length, start=half, into=grad_goals)
    return (loss_mean, grad_states, grad_goals)


def solution(mesh):
    spec = P("tm", "groups", None)
    return jax.shard_map(
        step,
        mesh=mesh,
        in_specs=(spec,) * 4,
        out_specs=(P("groups"), spec, spec),
        check_vma=False,
    )
```

profile of v0, /device:TPU:0, one launch (start us, length us, event | category | flops | bytes accessed | tf_op | source)
XLA Modules:
  0.0 90.6 jit_solution(3268242119098818901)
XLA Ops:
  0.6 3.1 %collective-permute-start.1 = (bf16[256,1024]{1,0:T(8,128)(2,1)}, bf16[256,1024]{1,0:T(8,128)(2,1)S(1)}, u32[]{:S(2)}, u32[]{:S(2)}) collective-permute-start(bf16[256,1024]{1,0:T(8,128)(2,1)} %bitcast.9), channel_id=1, source_target_pairs={{0,4},{1,5},{2,6},{3,7},{4,0},{5,1},{6,2},{7,3},{8,12},{9,13},{10,... | collective-permute-start | bytes 1572872 | tf_op jit(solution)/shard_map/ppermute | solution.py:16
  3.7 1.5 %collective-permute-start.3 = (bf16[256,1024]{1,0:T(8,128)(2,1)}, bf16[256,1024]{1,0:T(8,128)(2,1)S(1)}, u32[]{:S(2)}, u32[]{:S(2)}) collective-permute-start(bf16[256,1024]{1,0:T(8,128)(2,1)} %bitcast.10), channel_id=1, source_target_pairs={{0,2},{1,3},{2,0},{3,1},{4,6},{5,7},{6,4},{7,5},{8,10},{9,11},{10,... | collective-permute-start | bytes 1572872 | tf_op jit(solution)/shard_map/ppermute | solution.py:16
  5.3 0.7 collective-permute-start.6
  6.0 9.9 %collective-permute-done.1.refs_2_ = bf16[256,1024]{1,0:T(8,128)(2,1)S(1)} collective-permute-done((bf16[256,1024]{1,0:T(8,128)(2,1)}, bf16[256,1024]{1,0:T(8,128)(2,1)S(1)}, u32[]{:S(2)}, u32[]{:S(2)}) %collective-permute-start.1) | collective-permute-done | bytes 524320 | tf_op jit(solution)/shard_map/ppermute | solution.py:16
  15.9 1.7 %collective-permute-start.8 = (bf16[256,1024]{1,0:T(8,128)(2,1)S(1)}, bf16[256,1024]{1,0:T(8,128)(2,1)S(1)}, u32[]{:S(2)}, u32[]{:S(2)}) collective-permute-start(bf16[256,1024]{1,0:T(8,128)(2,1)S(1)} %collective-permute-done.1.refs_2_), channel_id=1, source_target_pairs={{0,2},{1,3},{2,0},{3,1},{4,6},{5,7},{6,4},{7,5},{8,10},{9,11},{10,... | collective-permute-start | bytes 1572872 | tf_op jit(solution)/shard_map/ppermute | solution.py:16
  17.6 5.5 %collective-permute-start.7 = (bf16[256,1024]{1,0:T(8,128)(2,1)}, bf16[256,1024]{1,0:T(8,128)(2,1)S(1)}, u32[]{:S(2)}, u32[]{:S(2)}) collective-permute-start(bf16[256,1024]{1,0:T(8,128)(2,1)} %bitcast.7), channel_id=1, source_target_pairs={{0,12},{1,13},{2,14},{3,15},{12,0},{13,1},{14,2},{15,3},{16,28},{1... | collective-permute-start | bytes 1572872 | tf_op jit(solution)/shard_map/ppermute | solution.py:16
  23.1 0.3 collective-permute-start.2
  23.4 0.3 collective-permute-start.4
  23.7 5.3 %collective-permute-done.8.refs_2_ = bf16[256,1024]{1,0:T(8,128)(2,1)S(1)} collective-permute-done((bf16[256,1024]{1,0:T(8,128)(2,1)S(1)}, bf16[256,1024]{1,0:T(8,128)(2,1)S(1)}, u32[]{:S(2)}, u32[]{:S(2)}) %collective-permute-start.8) | collective-permute-done | bytes 524320 | tf_op jit(solution)/shard_map/ppermute | solution.py:16
  29.0 0.7 add_bitcast_fusion
  29.6 0.1 convert_reduce_fusion.1
  29.7 0.7 convert_reduce_fusion
  30.5 1.0 %copy-done = bf16[256,1,1024]{2,0,1:T(8,128)(2,1)S(1)} copy-done((bf16[256,1,1024]{2,0,1:T(8,128)(2,1)S(1)}, bf16[256,1,1024]{2,0,1:T(8,128)(2,1)}, u32[]{:S(2)}) %copy-start) | copy-done | bytes 524312
  31.6 1.0 %copy-done.1 = bf16[256,1,1024]{2,0,1:T(8,128)(2,1)S(1)} copy-done((bf16[256,1,1024]{2,0,1:T(8,128)(2,1)S(1)}, bf16[256,1,1024]{2,0,1:T(8,128)(2,1)}, u32[]{:S(2)}) %copy-start.1) | copy-done | bytes 524312
  32.6 1.2 %shard_map.67 = (f32[8,128]{1,0:T(8,128)S(1)}, bf16[512,1024]{1,0:T(8,128)(2,1)S(1)}, bf16[2048,1024]{1,0:T(8,128)(2,1)S(1)}, bf16[2048,512]{1,0:T(8,128)(2,1)S(1)}) custom-call(s32[1]{0:T(128)} %bitcast.own_ref, f32[32]{0:T(128)S(1)} %pad_maximum_fusion.refs_0_, bf16[256,1024]{1,0:T(8,128)(2,1)S(1)} %bitcast.8, bf16[256,1024]{1,0:T(8,128)(2,1)S(1)} %bitcast.12), custom_call_target="tpu_custom_call" | custom-call | flops 134217728 | bytes 4194304 | tf_op jit(solution)/shard_map/pallas_call | solution.py:158
  33.8 2.1 %collective-permute-done.7 = bf16[256,1024]{1,0:T(8,128)(2,1)S(1)} collective-permute-done((bf16[256,1024]{1,0:T(8,128)(2,1)}, bf16[256,1024]{1,0:T(8,128)(2,1)S(1)}, u32[]{:S(2)}, u32[]{:S(2)}) %collective-permute-start.7) | collective-permute-done | bytes 524320 | tf_op jit(solution)/shard_map/ppermute | solution.py:16
  35.9 3.5 %collective-permute-start.5 = (f32[32]{0:T(128)S(1)}, f32[32]{0:T(128)S(1)}, u32[]{:S(2)}, u32[]{:S(2)}) collective-permute-start(f32[32]{0:T(128)S(1)} %pad_maximum_fusion.refs_0_), channel_id=1, source_target_pairs={{0,12},{1,13},{2,14},{3,15},{4,8},{5,9},{6,10},{7,11},{8,4},{9,5},... | collective-permute-start | bytes 392 | tf_op jit(solution)/shard_map/ppermute | solution.py:16
  39.4 0.2 add.38.refs_2_
  39.6 2.2 %shard_map.68 = (f32[8,128]{1,0:T(8,128)S(1)}, bf16[512,1024]{1,0:T(8,128)(2,1)S(1)}, bf16[2048,1024]{1,0:T(8,128)(2,1)S(1)}, bf16[2048,512]{1,0:T(8,128)(2,1)S(1)}) custom-call(s32[1]{0:T(128)} %bitcast.own_ref, f32[32]{0:T(128)S(1)} %pad_maximum_fusion.refs_0_, ...), custom_call_target="tpu_custom_call", output_to_operand_aliasing={{1}: (7, {}), {2}: (8, {}), {3}: (9, {})} | custom-call | flops 671088640 | bytes 4194304 | tf_op jit(solution)/shard_map/pallas_call | solution.py:158
  41.8 2.2 %shard_map.69 = (f32[8,128]{1,0:T(8,128)S(1)}, bf16[512,1024]{1,0:T(8,128)(2,1)S(1)}, bf16[2048,1024]{1,0:T(8,128)(2,1)S(1)}, bf16[2048,512]{1,0:T(8,128)(2,1)S(1)}) custom-call(s32[1]{0:T(128)} %bitcast.own_ref, f32[32]{0:T(128)S(1)} %pad_maximum_fusion.refs_0_, ...), custom_call_target="tpu_custom_call", output_to_operand_aliasing={{1}: (4, {}), {2}: (5, {}), {3}: (6, {})} | custom-call | flops 805306368 | bytes 4194304 | tf_op jit(solution)/shard_map/pallas_call | solution.py:158
  44.1 2.6 %shard_map.70 = (f32[8,128]{1,0:T(8,128)S(1)}, bf16[512,1024]{1,0:T(8,128)(2,1)S(1)}, bf16[2048,1024]{1,0:T(8,128)(2,1)S(1)}, bf16[2048,512]{1,0:T(8,128)(2,1)S(...) custom-call(s32[1]{0:T(128)} %bitcast.own_ref, ...), custom_call_target="tpu_custom_call", output_to_operand_aliasing={{1}: (5, {}), {2}: (6, {}), {3}: (7, {})} | custom-call | flops 1073741824 | bytes 4194304 | tf_op jit(solution)/shard_map/pallas_call | solution.py:158
  46.7 2.4 %shard_map.71 = (f32[256,1024]{1,0:T(8,128)S(1)}, bf16[256,1024]{1,0:T(8,128)(2,1)S(1)}, f32[256,1024]{1,0:T(8,128)S(1)}, bf16[256,1024]{1,0:T(8,128)(2,1)S(1)}, f32[256,1024]{1,0:T(8,128)S(1)}) custom-call(s32[1]{0:T(128)} %bitcast.own_ref, bf16[512,1024]{1,0:T(8,128)(2,1)S(1)} %get-tuple-element.43.refs_0_, ...), custom_call_target="tpu_custom_call" | custom-call | flops 2147483648 | bytes 4194304 | tf_op jit(solution)/shard_map/pallas_call | solution.py:158
  49.1 0.6 collective-permute-start.18
  49.7 0.7 shard_map.74
  50.4 0.1 collective-permute-start.16
  50.5 1.3 %shard_map.72 = bf16[256,1024]{1,0:T(8,128)(2,1)S(1)} custom-call(s32[1]{0:T(128)} %bitcast.own_ref, bf16[512,1024]{1,0:T(8,128)(2,1)S(1)} %get-tuple-element.43.refs_0_, bf16[2048,1024]{1,0:T(8,128)(2,1)S(1)} %get-tuple-element.44.refs_1_, bf16[2048,512]{1,0:T(8,128)(2,1)S(1)} %get-tuple-element.45.refs_2_), custom_call_target="tpu_custom_call" | custom-call | flops 1073741824 | bytes 4194304 | tf_op jit(solution)/shard_map/pallas_call | solution.py:158
  51.8 3.0 %collective-permute-start.14 = (bf16[256,1024]{1,0:T(8,128)(2,1)S(1)}, bf16[256,1024]{1,0:T(8,128)(2,1)S(1)}, u32[]{:S(2)}, u32[]{:S(2)}) collective-permute-start(bf16[256,1024]{1,0:T(8,128)(2,1)S(1)} %shard_map.72), channel_id=1, source_target_pairs={{0,12},{1,13},{2,14},{3,15},{4,8},{5,9},{6,10},{7,11},{8,4},{9,5},... | collective-permute-start | bytes 1572872 | tf_op jit(solution)/shard_map/ppermute | solution.py:16
  54.8 0.2 collective-permute-start.10
  55.0 1.0 %collective-permute-done.10 = f32[8,128]{1,0:T(8,128)S(1)} collective-permute-done((f32[8,128]{1,0:T(8,128)S(1)}, f32[8,128]{1,0:T(8,128)S(1)}, u32[]{:S(2)}, u32[]{:S(2)}) %collective-permute-start.10) | collective-permute-done | bytes 4128 | tf_op jit(solution)/shard_map/ppermute | solution.py:16
  56.0 0.5 collective-permute-start.11
  56.5 3.1 %collective-permute-done.11 = f32[8,128]{1,0:T(8,128)S(1)} collective-permute-done((f32[8,128]{1,0:T(8,128)S(1)}, f32[8,128]{1,0:T(8,128)S(1)}, u32[]{:S(2)}, u32[]{:S(2)}) %collective-permute-start.11) | collective-permute-done | bytes 4128 | tf_op jit(solution)/shard_map/ppermute | solution.py:16
  59.7 0.6 collective-permute-start.23
  60.3 6.5 %collective-permute-done.12 = f32[8,128]{1,0:T(8,128)S(1)} collective-permute-done((f32[8,128]{1,0:T(8,128)S(1)}, f32[8,128]{1,0:T(8,128)S(1)}, u32[]{:S(2)}, u32[]{:S(2)}) %collective-permute-start.12) | collective-permute-done | bytes 4128 | tf_op jit(solution)/shard_map/ppermute | solution.py:16
  66.8 0.5 collective-permute-start.20
  67.3 0.9 collective-permute-start.13
  68.3 1.6 %collective-permute-start.22 = (bf16[128,1024]{1,0:T(8,128)(2,1)S(1)}, bf16[128,1024]{1,0:T(8,128)(2,1)S(1)}, u32[]{:S(2)}, u32[]{:S(2)}) collective-permute-start(bf16[128,1024]{1,0:T(8,128)(2,1)S(1)} %shard_map.78), channel_id=1, source_target_pairs={{0,2},{1,3},{2,0},{3,1},{4,6},{5,7},{6,4},{7,5},{8,10},{9,11},{10,... | collective-permute-start | bytes 786440 | tf_op jit(solution)/shard_map/ppermute | solution.py:16
  69.9 0.1 shard_map.80
  70.0 6.0 %collective-permute-done.20.refs_2_ = bf16[128,1024]{1,0:T(8,128)(2,1)S(1)} collective-permute-done((bf16[128,1024]{1,0:T(8,128)(2,1)S(1)}, bf16[128,1024]{1,0:T(8,128)(2,1)S(1)}, u32[]{:S(2)}, u32[]{:S(2)}) %collective-permute-start.20) | collective-permute-done | bytes 262176 | tf_op jit(solution)/shard_map/ppermute | solution.py:16
  76.0 2.5 %collective-permute-start.24 = (bf16[128,1024]{1,0:T(8,128)(2,1)S(1)}, bf16[128,1024]{1,0:T(8,128)(2,1)S(1)}, u32[]{:S(2)}, u32[]{:S(2)}) collective-permute-start(bf16[128,1024]{1,0:T(8,128)(2,1)S(1)} %shard_map.80), channel_id=1, source_target_pairs={{0,4},{1,5},{2,6},{3,7},{4,0},{5,1},{6,2},{7,3},{8,12},{9,13},{10,... | collective-permute-start | bytes 786440 | tf_op jit(solution)/shard_map/ppermute | solution.py:16
  78.5 0.1 shard_map.77
  78.6 0.6 collective-permute-start.17
  79.2 1.6 %shard_map.73 = (f32[1]{0:T(128)}, f32[256,1,1024]{2,1,0:T(1,128)}) custom-call(f32[8,128]{1,0:T(8,128)S(1)} %add.43.refs_0_, f32[8,128]{1,0:T(8,128)S(1)} %collective-permute-done.13.refs_1_, f32[256,1024]{1,0:T(8,128)S(1)} %get-tuple-element.46.refs_2_, bf16[256,1024]{1,0:T(8,128)(2,1)S(1)} %collective-permute-done.14.refs_3_), custom_call_target="tpu_custom_call" | custom-call | flops 1048576 | bytes 3670016 | tf_op jit(solution)/shard_map/pallas_call | solution.py:237
  80.8 0.8 collective-permute-done.22.refs_2_
  81.6 4.0 %collective-permute-done.24.refs_3_ = bf16[128,1024]{1,0:T(8,128)(2,1)S(1)} collective-permute-done((bf16[128,1024]{1,0:T(8,128)(2,1)S(1)}, bf16[128,1024]{1,0:T(8,128)(2,1)S(1)}, u32[]{:S(2)}, u32[]{:S(2)}) %collective-permute-start.24) | collective-permute-done | bytes 262176 | tf_op jit(solution)/shard_map/ppermute | solution.py:16
  85.6 0.9 shard_map.81.refs_4_
  86.5 0.3 collective-permute-done.17.refs_2_
  86.8 3.0 %collective-permute-done.21.refs_3_ = bf16[128,1024]{1,0:T(8,128)(2,1)S(1)} collective-permute-done((bf16[128,1024]{1,0:T(8,128)(2,1)S(1)}, bf16[128,1024]{1,0:T(8,128)(2,1)S(1)}, u32[]{:S(2)}, u32[]{:S(2)}) %collective-permute-start.21) | collective-permute-done | bytes 262176 | tf_op jit(solution)/shard_map/ppermute | solution.py:16
  89.8 0.9 shard_map.82
  (31 shorter events, 0.4 us)
Async XLA Ops:
  0.6 15.3 %collective-permute-start.1 = (bf16[256,1024]{1,0:T(8,128)(2,1)}, bf16[256,1024]{1,0:T(8,128)(2,1)S(1)}, u32[]{:S(2)}, u32[]{:S(2)}) collective-permute-start(bf16[256,1024]{1,0:T(8,128)(2,1)} %bitcast.9), channel_id=1, source_target_pairs={{0,4},{1,5},{2,6},{3,7},{4,0},{5,1},{6,2},{7,3},{8,12},{9,13},{10,... | collective-permute-start | bytes 1572872 | tf_op jit(solution)/shard_map/ppermute | solution.py:16
  3.7 19.3 %collective-permute-start.3 = (bf16[256,1024]{1,0:T(8,128)(2,1)}, bf16[256,1024]{1,0:T(8,128)(2,1)S(1)}, u32[]{:S(2)}, u32[]{:S(2)}) collective-permute-start(bf16[256,1024]{1,0:T(8,128)(2,1)} %bitcast.10), channel_id=1, source_target_pairs={{0,2},{1,3},{2,0},{3,1},{4,6},{5,7},{6,4},{7,5},{8,10},{9,11},{10,... | collective-permute-start | bytes 1572872 | tf_op jit(solution)/shard_map/ppermute | solution.py:16
  5.3 18.1 %collective-permute-start.6 = (bf16[256,1024]{1,0:T(8,128)(2,1)}, bf16[256,1024]{1,0:T(8,128)(2,1)S(1)}, u32[]{:S(2)}, u32[]{:S(2)}) collective-permute-start(bf16[256,1024]{1,0:T(8,128)(2,1)} %bitcast.6), channel_id=1, source_target_pairs={{4,8},{5,9},{6,10},{7,11},{8,4},{9,5},{10,6},{11,7},{20,24},{21,25... | collective-permute-start | bytes 1572872 | tf_op jit(solution)/shard_map/ppermute | solution.py:16
  15.9 13.1 %collective-permute-start.8 = (bf16[256,1024]{1,0:T(8,128)(2,1)S(1)}, bf16[256,1024]{1,0:T(8,128)(2,1)S(1)}, u32[]{:S(2)}, u32[]{:S(2)}) collective-permute-start(bf16[256,1024]{1,0:T(8,128)(2,1)S(1)} %collective-permute-done.1.refs_2_), channel_id=1, source_target_pairs={{0,2},{1,3},{2,0},{3,1},{4,6},{5,7},{6,4},{7,5},{8,10},{9,11},{10,... | collective-permute-start | bytes 1572872 | tf_op jit(solution)/shard_map/ppermute | solution.py:16
  17.6 22.0 %collective-permute-start = (bf16[256,1024]{1,0:T(8,128)(2,1)}, bf16[256,1024]{1,0:T(8,128)(2,1)S(1)}, u32[]{:S(2)}, u32[]{:S(2)}) collective-permute-start(bf16[256,1024]{1,0:T(8,128)(2,1)} %bitcast.11), channel_id=1, source_target_pairs={{0,1},{1,0},{2,3},{3,2},{4,5},{5,4},{6,7},{7,6},{8,9},{9,8},{10,11... | collective-permute-start | bytes 1572872 | tf_op jit(solution)/shard_map/ppermute | solution.py:16
  17.6 18.3 %collective-permute-start.7 = (bf16[256,1024]{1,0:T(8,128)(2,1)}, bf16[256,1024]{1,0:T(8,128)(2,1)S(1)}, u32[]{:S(2)}, u32[]{:S(2)}) collective-permute-start(bf16[256,1024]{1,0:T(8,128)(2,1)} %bitcast.7), channel_id=1, source_target_pairs={{0,12},{1,13},{2,14},{3,15},{12,0},{13,1},{14,2},{15,3},{16,28},{1... | collective-permute-start | bytes 1572872 | tf_op jit(solution)/shard_map/ppermute | solution.py:16
  23.1 16.5 %collective-permute-start.2 = (bf16[256,1024]{1,0:T(8,128)(2,1)S(1)}, bf16[256,1024]{1,0:T(8,128)(2,1)S(1)}, u32[]{:S(2)}, u32[]{:S(2)}) collective-permute-start(bf16[256,1024]{1,0:T(8,128)(2,1)S(1)} %collective-permute-done.1.refs_2_), channel_id=1, source_target_pairs={{0,1},{1,0},{2,3},{3,2},{4,5},{5,4},{6,7},{7,6},{8,9},{9,8},{10,11... | collective-permute-start | bytes 1572872 | tf_op jit(solution)/shard_map/ppermute | solution.py:16
  23.4 16.2 %collective-permute-start.4 = (bf16[256,1024]{1,0:T(8,128)(2,1)S(1)}, bf16[256,1024]{1,0:T(8,128)(2,1)S(1)}, u32[]{:S(2)}, u32[]{:S(2)}) collective-permute-start(bf16[256,1024]{1,0:T(8,128)(2,1)S(1)} %collective-permute-done.3.refs_4_), channel_id=1, source_target_pairs={{0,1},{1,0},{2,3},{3,2},{4,5},{5,4},{6,7},{7,6},{8,9},{9,8},{10,11... | collective-permute-start | bytes 1572872 | tf_op jit(solution)/shard_map/ppermute | solution.py:16
  29.0 15.1 %collective-permute-start.9 = (bf16[256,1024]{1,0:T(8,128)(2,1)S(1)}, bf16[256,1024]{1,0:T(8,128)(2,1)S(1)}, u32[]{:S(2)}, u32[]{:S(2)}) collective-permute-start(bf16[256,1024]{1,0:T(8,128)(2,1)S(1)} %collective-permute-done.8.refs_2_), channel_id=1, source_target_pairs={{0,1},{1,0},{2,3},{3,2},{4,5},{5,4},{6,7},{7,6},{8,9},{9,8},{10,11... | collective-permute-start | bytes 1572872 | tf_op jit(solution)/shard_map/ppermute | solution.py:16
  30.5 1.0 %copy-start = (bf16[256,1,1024]{2,0,1:T(8,128)(2,1)S(1)}, bf16[256,1,1024]{2,0,1:T(8,128)(2,1)}, u32[]{:S(2)}) copy-start(bf16[256,1,1024]{2,0,1:T(8,128)(2,1)} %param.4) | copy-start | bytes 1572868
  31.6 1.0 %copy-start.1 = (bf16[256,1,1024]{2,0,1:T(8,128)(2,1)S(1)}, bf16[256,1,1024]{2,0,1:T(8,128)(2,1)}, u32[]{:S(2)}) copy-start(bf16[256,1,1024]{2,0,1:T(8,128)(2,1)} %param.5) | copy-start | bytes 1572868
  35.9 5.9 %collective-permute-start.5 = (f32[32]{0:T(128)S(1)}, f32[32]{0:T(128)S(1)}, u32[]{:S(2)}, u32[]{:S(2)}) collective-permute-start(f32[32]{0:T(128)S(1)} %pad_maximum_fusion.refs_0_), channel_id=1, source_target_pairs={{0,12},{1,13},{2,14},{3,15},{4,8},{5,9},{6,10},{7,11},{8,4},{9,5},... | collective-permute-start | bytes 392 | tf_op jit(solution)/shard_map/ppermute | solution.py:16
  46.6 13.0 %collective-permute-start.19 = (bf16[256,1024]{1,0:T(8,128)(2,1)S(1)}, bf16[256,1024]{1,0:T(8,128)(2,1)S(1)}, u32[]{:S(2)}, u32[]{:S(2)}) collective-permute-start(bf16[256,1024]{1,0:T(8,128)(2,1)S(1)} %get-tuple-element.56), channel_id=1, source_target_pairs={{0,1},{1,0},{2,3},{3,2},{4,5},{5,4},{6,7},{7,6},{8,9},{9,8},{10,11... | collective-permute-start | bytes 1572872 | tf_op jit(solution)/shard_map/ppermute | solution.py:16
  49.1 17.7 %collective-permute-start.18 = (bf16[256,1024]{1,0:T(8,128)(2,1)S(1)}, bf16[256,1024]{1,0:T(8,128)(2,1)S(1)}, u32[]{:S(2)}, u32[]{:S(2)}) collective-permute-start(bf16[256,1024]{1,0:T(8,128)(2,1)S(1)} %get-tuple-element.54), channel_id=1, source_target_pairs={{0,1},{1,0},{2,3},{3,2},{4,5},{5,4},{6,7},{7,6},{8,9},{9,8},{10,11... | collective-permute-start | bytes 1572872 | tf_op jit(solution)/shard_map/ppermute | solution.py:16
  50.4 16.9 %collective-permute-start.16 = (bf16[256,1024]{1,0:T(8,128)(2,1)S(1)}, bf16[256,1024]{1,0:T(8,128)(2,1)S(1)}, u32[]{:S(2)}, u32[]{:S(2)}) collective-permute-start(bf16[256,1024]{1,0:T(8,128)(2,1)S(1)} %get-tuple-element.52), channel_id=1, source_target_pairs={{0,1},{1,0},{2,3},{3,2},{4,5},{5,4},{6,7},{7,6},{8,9},{9,8},{10,11... | collective-permute-start | bytes 1572872 | tf_op jit(solution)/shard_map/ppermute | solution.py:16
  51.8 27.4 %collective-permute-start.14 = (bf16[256,1024]{1,0:T(8,128)(2,1)S(1)}, bf16[256,1024]{1,0:T(8,128)(2,1)S(1)}, u32[]{:S(2)}, u32[]{:S(2)}) collective-permute-start(bf16[256,1024]{1,0:T(8,128)(2,1)S(1)} %shard_map.72), channel_id=1, source_target_pairs={{0,12},{1,13},{2,14},{3,15},{4,8},{5,9},{6,10},{7,11},{8,4},{9,5},... | collective-permute-start | bytes 1572872 | tf_op jit(solution)/shard_map/ppermute | solution.py:16
  54.8 1.2 %collective-permute-start.10 = (f32[8,128]{1,0:T(8,128)S(1)}, f32[8,128]{1,0:T(8,128)S(1)}, u32[]{:S(2)}, u32[]{:S(2)}) collective-permute-start(f32[8,128]{1,0:T(8,128)S(1)} %add_add_fusion), channel_id=1, source_target_pairs={{0,1},{1,0},{2,3},{3,2},{4,5},{5,4},{6,7},{7,6},{8,9},{9,8},{10,11... | collective-permute-start | bytes 12296 | tf_op jit(solution)/shard_map/ppermute | solution.py:16
  56.0 3.6 %collective-permute-start.11 = (f32[8,128]{1,0:T(8,128)S(1)}, f32[8,128]{1,0:T(8,128)S(1)}, u32[]{:S(2)}, u32[]{:S(2)}) collective-permute-start(f32[8,128]{1,0:T(8,128)S(1)} %add.41), channel_id=1, source_target_pairs={{0,2},{1,3},{2,0},{3,1},{4,6},{5,7},{6,4},{7,5},{8,10},{9,11},{10,... | collective-permute-start | bytes 12296 | tf_op jit(solution)/shard_map/ppermute | solution.py:16
  59.6 7.2 %collective-permute-start.12 = (f32[8,128]{1,0:T(8,128)S(1)}, f32[8,128]{1,0:T(8,128)S(1)}, u32[]{:S(2)}, u32[]{:S(2)}) collective-permute-start(f32[8,128]{1,0:T(8,128)S(1)} %add.42), channel_id=1, source_target_pairs={{0,4},{1,5},{2,6},{3,7},{4,0},{5,1},{6,2},{7,3},{8,12},{9,13},{10,... | collective-permute-start | bytes 12296 | tf_op jit(solution)/shard_map/ppermute | solution.py:16
  59.7 8.7 %collective-permute-start.23 = (bf16[128,1024]{1,0:T(8,128)(2,1)S(1)}, bf16[128,1024]{1,0:T(8,128)(2,1)S(1)}, u32[]{:S(2)}, u32[]{:S(2)}) collective-permute-start(bf16[128,1024]{1,0:T(8,128)(2,1)S(1)} %shard_map.79), channel_id=1, source_target_pairs={{0,2},{1,3},{2,0},{3,1},{4,6},{5,7},{6,4},{7,5},{8,10},{9,11},{10,... | collective-permute-start | bytes 786440 | tf_op jit(solution)/shard_map/ppermute | solution.py:16
  66.8 14.0 %collective-permute-start.15 = (bf16[256,1024]{1,0:T(8,128)(2,1)S(1)}, bf16[256,1024]{1,0:T(8,128)(2,1)S(1)}, u32[]{:S(2)}, u32[]{:S(2)}) collective-permute-start(bf16[256,1024]{1,0:T(8,128)(2,1)S(1)} %get-tuple-element.50), channel_id=1, source_target_pairs={{0,1},{1,0},{2,3},{3,2},{4,5},{5,4},{6,7},{7,6},{8,9},{9,8},{10,11... | collective-permute-start | bytes 1572872 | tf_op jit(solution)/shard_map/ppermute | solution.py:16
  66.8 9.2 %collective-permute-start.20 = (bf16[128,1024]{1,0:T(8,128)(2,1)S(1)}, bf16[128,1024]{1,0:T(8,128)(2,1)S(1)}, u32[]{:S(2)}, u32[]{:S(2)}) collective-permute-start(bf16[128,1024]{1,0:T(8,128)(2,1)S(1)} %shard_map.76), channel_id=1, source_target_pairs={{0,2},{1,3},{2,0},{3,1},{4,6},{5,7},{6,4},{7,5},{8,10},{9,11},{10,... | collective-permute-start | bytes 786440 | tf_op jit(solution)/shard_map/ppermute | solution.py:16
  67.3 11.2 %collective-permute-start.13 = (f32[8,128]{1,0:T(8,128)S(1)}, f32[8,128]{1,0:T(8,128)S(1)}, u32[]{:S(2)}, u32[]{:S(2)}) collective-permute-start(f32[8,128]{1,0:T(8,128)S(1)} %add.43.refs_0_), channel_id=1, source_target_pairs={{0,12},{1,13},{2,14},{3,15},{4,8},{5,9},{6,10},{7,11},{8,4},{9,5},... | collective-permute-start | bytes 12296 | tf_op jit(solution)/shard_map/ppermute | solution.py:16
  68.3 13.3 %collective-permute-start.22 = (bf16[128,1024]{1,0:T(8,128)(2,1)S(1)}, bf16[128,1024]{1,0:T(8,128)(2,1)S(1)}, u32[]{:S(2)}, u32[]{:S(2)}) collective-permute-start(bf16[128,1024]{1,0:T(8,128)(2,1)S(1)} %shard_map.78), channel_id=1, source_target_pairs={{0,2},{1,3},{2,0},{3,1},{4,6},{5,7},{6,4},{7,5},{8,10},{9,11},{10,... | collective-permute-start | bytes 786440 | tf_op jit(solution)/shard_map/ppermute | solution.py:16
  76.0 9.6 %collective-permute-start.24 = (bf16[128,1024]{1,0:T(8,128)(2,1)S(1)}, bf16[128,1024]{1,0:T(8,128)(2,1)S(1)}, u32[]{:S(2)}, u32[]{:S(2)}) collective-permute-start(bf16[128,1024]{1,0:T(8,128)(2,1)S(1)} %shard_map.80), channel_id=1, source_target_pairs={{0,4},{1,5},{2,6},{3,7},{4,0},{5,1},{6,2},{7,3},{8,12},{9,13},{10,... | collective-permute-start | bytes 786440 | tf_op jit(solution)/shard_map/ppermute | solution.py:16
  78.6 8.2 %collective-permute-start.17 = (bf16[128,1024]{1,0:T(8,128)(2,1)S(1)}, bf16[128,1024]{1,0:T(8,128)(2,1)S(1)}, u32[]{:S(2)}, u32[]{:S(2)}) collective-permute-start(bf16[128,1024]{1,0:T(8,128)(2,1)S(1)} %shard_map.75), channel_id=1, source_target_pairs={{0,2},{1,3},{2,0},{3,1},{4,6},{5,7},{6,4},{7,5},{8,10},{9,11},{10,... | collective-permute-start | bytes 786440 | tf_op jit(solution)/shard_map/ppermute | solution.py:16
  79.2 10.6 %collective-permute-start.21 = (bf16[128,1024]{1,0:T(8,128)(2,1)S(1)}, bf16[128,1024]{1,0:T(8,128)(2,1)S(1)}, u32[]{:S(2)}, u32[]{:S(2)}) collective-permute-start(bf16[128,1024]{1,0:T(8,128)(2,1)S(1)} %shard_map.77), channel_id=1, source_target_pairs={{0,4},{1,5},{2,6},{3,7},{4,0},{5,1},{6,2},{7,3},{8,12},{9,13},{10,... | collective-permute-start | bytes 786440 | tf_op jit(solution)/shard_map/ppermute | solution.py:16
where the time goes:
time: 90.9 us; the launch traced here: 90.6 us
  waiting for transfers between devices  42 us (46%)
  starting transfers between devices  27.7 us (30%)
  Pallas kernels  16.2 us (18%)
  local copies, waits for them, and re-layouts  2.08 us (2%)
  other arithmetic  1.77 us (2%)
    ppermute x25, waiting for transfers between devices, swap(): lax.ppermute(value, AXIS, [(i, i ^ offset) for i in range(size) if only(i)])  42 us
    ppermute x25, starting transfers between devices, swap(): lax.ppermute(value, AXIS, [(i, i ^ offset) for i in range(size) if only(i)])  27.7 us
    pallas_call x7, Pallas kernels, phase(): pl.pallas_call(functools.partial(tile_kernel, plan), in_specs=in_specs, o...  12.5 us
    pallas_call x3, Pallas kernels, finish_rows(): pl.pallas_call(functools.partial(finish_kernel, len(losses), [first for _...  3.36 us
    unnamed x4, local copies, waits for them, and re-layouts  2.08 us
  transfers between devices with their start and end apart: 25, of which 11 were waited for; matrix products, arithmetic and copies ran while one was open for 2% of the time, Pallas kernels for 14%

commit v1 on v0

--- a/solution.py
+++ b/solution.py
@@ -212,15 +212,15 @@
     n_part = len(firsts)
     losses, parts, refs = refs[:n_loss], refs[n_loss : n_loss + n_part], refs[n_loss + n_part + in_place :]
     *outs, total, sem = refs
-    if n_loss:
-        outs[-2][0] = jnp.sum(sum(loss[...] for loss in losses)) * (1.0 / count)
-    rows, n, stores = total.shape[0], 64, []
+    rows, n, stores = total.shape[0], 32, []
     for r in range(0, rows, n):
         here = pl.ds(r, n)
         total[here, :] = sum(part[f + r : f + r + n, :].astype(jnp.float32) for f, part in zip(firsts, parts))
         there = outs[-1].at[pl.ds(start + r, n), 0, :]
         stores.append(pltpu.make_async_copy(total.at[here], there, sem.at[len(stores)]))
         stores[-1].start()
+    if n_loss:
+        outs[-2][0] = jnp.sum(sum(loss[...] for loss in losses)) * (1.0 / count)
     for copy in stores:
         copy.wait()
 
@@ -240,7 +240,7 @@
         out_specs=out_specs,
         out_shape=out_shape,
         input_output_aliases={len(held): len(out_shape) - 1} if in_place else {},
-        scratch_shapes=[pltpu.VMEM((rows, width), jnp.float32), pltpu.SemaphoreType.DMA((rows // 64,))],
+        scratch_shapes=[pltpu.VMEM((rows, width), jnp.float32), pltpu.SemaphoreType.DMA((rows // 32,))],
         cost_estimate=pl.CostEstimate(flops=4 * rows * width, bytes_accessed=14 * rows * width, transcendentals=0),
         compiler_params=pltpu.CompilerParams(vmem_limit_bytes=8 << 20),
     )(*held, *([into] if in_place else []))
@@ -288,10 +288,10 @@
         return {p: c for p, c in cols.items() if start <= p < end}
 
     loss_a, held, _, _ = phase(
-        own, tables[:1], {0: state}, arrived(0, length), None, new=[(0, length, 0, length)], **fixed
+        own, tables[:1], {0: state}, arrived(0, 2 * length), None, new=[(0, length, 0, 2 * length)], **fixed
     )
     loss_b, held, _, _ = phase(
-        own, tables[:1], {}, arrived(length, last), held, new=[(0, length, length, last)], **fixed
+        own, tables[:1], {}, arrived(2 * length, last), held, new=[(0, length, 2 * length, last)], **fixed
     )
     loss_c, held, _, _ = phase(own, tables, {length: pair}, {}, held, new=[(length, n_row, 0, last)], **fixed)
     sides, own_sums = {}, {}

time: 90.9 us -> 91.4 us (level)
  no operation moved by 1% of the time
where the time goes in v1:
time: 91.4 us; the launch traced here: 91.2 us
  waiting for transfers between devices  42.6 us (47%)
  starting transfers between devices  27.7 us (30%)
  Pallas kernels  16.1 us (18%)
  local copies, waits for them, and re-layouts  2.08 us (2%)
  other arithmetic  1.77 us (2%)
    ppermute x25, waiting for transfers between devices, swap(): lax.ppermute(value, AXIS, [(i, i ^ offset) for i in range(size) if only(i)])  42.6 us
    ppermute x25, starting transfers between devices, swap(): lax.ppermute(value, AXIS, [(i, i ^ offset) for i in range(size) if only(i)])  27.7 us
    pallas_call x7, Pallas kernels, phase(): pl.pallas_call(functools.partial(tile_kernel, plan), in_specs=in_specs, o...  12.5 us
    pallas_call x3, Pallas kernels, finish_rows(): pl.pallas_call(functools.partial(finish_kernel, len(losses), [first for _...  3.25 us
    unnamed x4, local copies, waits for them, and re-layouts  2.08 us
  transfers between devices with their start and end apart: 25, of which 11 were waited for; matrix products, arithmetic and copies ran while one was open for 2% of the time, Pallas kernels for 14%

profile of v1, /device:TPU:0, one launch (start us, length us, event | category | flops | bytes accessed | tf_op | source)
XLA Modules:
  0.0 91.2 jit_solution(11473479713428453922)
XLA Ops:
  0.6 3.1 %collective-permute-start.1 = (bf16[256,1024]{1,0:T(8,128)(2,1)}, bf16[256,1024]{1,0:T(8,128)(2,1)S(1)}, u32[]{:S(2)}, u32[]{:S(2)}) collective-permute-start(bf16[256,1024]{1,0:T(8,128)(2,1)} %bitcast.6), channel_id=1, source_target_pairs={{0,4},{1,5},{2,6},{3,7},{4,0},{5,1},{6,2},{7,3},{8,12},{9,13},{10,... | collective-permute-start | bytes 1572872 | tf_op jit(solution)/shard_map/ppermute | solution.py:16
  3.7 1.5 %collective-permute-start.3 = (bf16[256,1024]{1,0:T(8,128)(2,1)}, bf16[256,1024]{1,0:T(8,128)(2,1)S(1)}, u32[]{:S(2)}, u32[]{:S(2)}) collective-permute-start(bf16[256,1024]{1,0:T(8,128)(2,1)} %bitcast.7), channel_id=1, source_target_pairs={{0,2},{1,3},{2,0},{3,1},{4,6},{5,7},{6,4},{7,5},{8,10},{9,11},{10,... | collective-permute-start | bytes 1572872 | tf_op jit(solution)/shard_map/ppermute | solution.py:16
  5.3 0.7 collective-permute-start.6
  6.0 9.9 %collective-permute-done.1.refs_1_ = bf16[256,1024]{1,0:T(8,128)(2,1)S(1)} collective-permute-done((bf16[256,1024]{1,0:T(8,128)(2,1)}, bf16[256,1024]{1,0:T(8,128)(2,1)S(1)}, u32[]{:S(2)}, u32[]{:S(2)}) %collective-permute-start.1) | collective-permute-done | bytes 524320 | tf_op jit(solution)/shard_map/ppermute | solution.py:16
  15.9 1.7 %collective-permute-start.8 = (bf16[256,1024]{1,0:T(8,128)(2,1)S(1)}, bf16[256,1024]{1,0:T(8,128)(2,1)S(1)}, u32[]{:S(2)}, u32[]{:S(2)}) collective-permute-start(bf16[256,1024]{1,0:T(8,128)(2,1)S(1)} %collective-permute-done.1.refs_1_), channel_id=1, source_target_pairs={{0,2},{1,3},{2,0},{3,1},{4,6},{5,7},{6,4},{7,5},{8,10},{9,11},{10,... | collective-permute-start | bytes 1572872 | tf_op jit(solution)/shard_map/ppermute | solution.py:16
  17.6 5.5 %collective-permute-start.7 = (bf16[256,1024]{1,0:T(8,128)(2,1)}, bf16[256,1024]{1,0:T(8,128)(2,1)S(1)}, u32[]{:S(2)}, u32[]{:S(2)}) collective-permute-start(bf16[256,1024]{1,0:T(8,128)(2,1)} %bitcast.11), channel_id=1, source_target_pairs={{0,12},{1,13},{2,14},{3,15},{12,0},{13,1},{14,2},{15,3},{16,28},{1... | collective-permute-start | bytes 1572872 | tf_op jit(solution)/shard_map/ppermute | solution.py:16
  23.1 0.3 collective-permute-start.2
  23.4 0.3 collective-permute-start.4
  23.7 5.3 %collective-permute-done.8.refs_2_ = bf16[256,1024]{1,0:T(8,128)(2,1)S(1)} collective-permute-done((bf16[256,1024]{1,0:T(8,128)(2,1)S(1)}, bf16[256,1024]{1,0:T(8,128)(2,1)S(1)}, u32[]{:S(2)}, u32[]{:S(2)}) %collective-permute-start.8) | collective-permute-done | bytes 524320 | tf_op jit(solution)/shard_map/ppermute | solution.py:16
  29.0 0.7 add_bitcast_fusion
  29.6 0.1 convert_reduce_fusion.1
  29.7 0.7 convert_reduce_fusion
  30.5 5.3 %collective-permute-done.7 = bf16[256,1024]{1,0:T(8,128)(2,1)S(1)} collective-permute-done((bf16[256,1024]{1,0:T(8,128)(2,1)}, bf16[256,1024]{1,0:T(8,128)(2,1)S(1)}, u32[]{:S(2)}, u32[]{:S(2)}) %collective-permute-start.7) | collective-permute-done | bytes 524320 | tf_op jit(solution)/shard_map/ppermute | solution.py:16
  35.9 3.5 %collective-permute-start.5 = (f32[32]{0:T(128)S(1)}, f32[32]{0:T(128)S(1)}, u32[]{:S(2)}, u32[]{:S(2)}) collective-permute-start(f32[32]{0:T(128)S(1)} %pad_maximum_fusion.refs_0_), channel_id=1, source_target_pairs={{0,12},{1,13},{2,14},{3,15},{4,8},{5,9},{6,10},{7,11},{8,4},{9,5},... | collective-permute-start | bytes 392 | tf_op jit(solution)/shard_map/ppermute | solution.py:16
  39.4 0.2 add.38.refs_2_
  39.6 1.0 %copy-done = bf16[256,1,1024]{2,0,1:T(8,128)(2,1)S(1)} copy-done((bf16[256,1,1024]{2,0,1:T(8,128)(2,1)S(1)}, bf16[256,1,1024]{2,0,1:T(8,128)(2,1)}, u32[]{:S(2)}) %copy-start) | copy-done | bytes 524312
  40.7 1.0 %copy-done.1 = bf16[256,1,1024]{2,0,1:T(8,128)(2,1)S(1)} copy-done((bf16[256,1,1024]{2,0,1:T(8,128)(2,1)S(1)}, bf16[256,1,1024]{2,0,1:T(8,128)(2,1)}, u32[]{:S(2)}) %copy-start.1) | copy-done | bytes 524312
  41.7 1.4 %shard_map.67 = (f32[8,128]{1,0:T(8,128)S(1)}, bf16[512,1024]{1,0:T(8,128)(2,1)S(1)}, bf16[2048,1024]{1,0:T(8,128)(2,1)S(1)}, bf16[2048,512]{1,0:T(8,128)(2,1)S(1)}) custom-call(s32[1]{0:T(128)} %bitcast.own_ref, f32[32]{0:T(128)S(1)} %pad_maximum_fusion.refs_0_, bf16[256,1024]{1,0:T(8,128)(2,1)S(1)} %bitcast.12, bf16[256,1024]{1,0:T(8,128)(2,1)S(1)} %bitcast.9, ...), custom_call_target="tpu_custom_call" | custom-call | flops 268435456 | bytes 4194304 | tf_op jit(solution)/shard_map/pallas_call | solution.py:158
  43.2 1.9 %shard_map.68 = (f32[8,128]{1,0:T(8,128)S(1)}, bf16[512,1024]{1,0:T(8,128)(2,1)S(1)}, bf16[2048,1024]{1,0:T(8,128)(2,1)S(1)}, bf16[2048,512]{1,0:T(8,128)(2,1)S(1)}) custom-call(s32[1]{0:T(128)} %bitcast.own_ref, f32[32]{0:T(128)S(1)} %pad_maximum_fusion.refs_0_, ...), custom_call_target="tpu_custom_call", output_to_operand_aliasing={{1}: (6, {}), {2}: (7, {}), {3}: (8, {})} | custom-call | flops 536870912 | bytes 4194304 | tf_op jit(solution)/shard_map/pallas_call | solution.py:158
  45.0 2.2 %shard_map.69 = (f32[8,128]{1,0:T(8,128)S(1)}, bf16[512,1024]{1,0:T(8,128)(2,1)S(1)}, bf16[2048,1024]{1,0:T(8,128)(2,1)S(1)}, bf16[2048,512]{1,0:T(8,128)(2,1)S(1)}) custom-call(s32[1]{0:T(128)} %bitcast.own_ref, f32[32]{0:T(128)S(1)} %pad_maximum_fusion.refs_0_, ...), custom_call_target="tpu_custom_call", output_to_operand_aliasing={{1}: (4, {}), {2}: (5, {}), {3}: (6, {})} | custom-call | flops 805306368 | bytes 4194304 | tf_op jit(solution)/shard_map/pallas_call | solution.py:158
  47.3 2.6 %shard_map.70 = (f32[8,128]{1,0:T(8,128)S(1)}, bf16[512,1024]{1,0:T(8,128)(2,1)S(1)}, bf16[2048,1024]{1,0:T(8,128)(2,1)S(1)}, bf16[2048,512]{1,0:T(8,128)(2,1)S(...) custom-call(s32[1]{0:T(128)} %bitcast.own_ref, ...), custom_call_target="tpu_custom_call", output_to_operand_aliasing={{1}: (5, {}), {2}: (6, {}), {3}: (7, {})} | custom-call | flops 1073741824 | bytes 4194304 | tf_op jit(solution)/shard_map/pallas_call | solution.py:158
  49.9 2.4 %shard_map.71 = (f32[256,1024]{1,0:T(8,128)S(1)}, bf16[256,1024]{1,0:T(8,128)(2,1)S(1)}, f32[256,1024]{1,0:T(8,128)S(1)}, bf16[256,1024]{1,0:T(8,128)(2,1)S(1)}, f32[256,1024]{1,0:T(8,128)S(1)}) custom-call(s32[1]{0:T(128)} %bitcast.own_ref, bf16[512,1024]{1,0:T(8,128)(2,1)S(1)} %get-tuple-element.43.refs_0_, ...), custom_call_target="tpu_custom_call" | custom-call | flops 2147483648 | bytes 4194304 | tf_op jit(solution)/shard_map/pallas_call | solution.py:158
  52.3 0.6 collective-permute-start.18
  52.9 0.7 shard_map.74
  53.6 0.1 collective-permute-start.16
  53.7 1.3 %shard_map.72 = bf16[256,1024]{1,0:T(8,128)(2,1)S(1)} custom-call(s32[1]{0:T(128)} %bitcast.own_ref, bf16[512,1024]{1,0:T(8,128)(2,1)S(1)} %get-tuple-element.43.refs_0_, bf16[2048,1024]{1,0:T(8,128)(2,1)S(1)} %get-tuple-element.44.refs_1_, bf16[2048,512]{1,0:T(8,128)(2,1)S(1)} %get-tuple-element.45.refs_2_), custom_call_target="tpu_custom_call" | custom-call | flops 1073741824 | bytes 4194304 | tf_op jit(solution)/shard_map/pallas_call | solution.py:158
  55.0 0.3 collective-permute-start.14
  55.4 0.3 collective-permute-start.10
  55.7 0.9 collective-permute-done.10
  56.5 0.5 collective-permute-start.11
  57.1 3.1 %collective-permute-done.11 = f32[8,128]{1,0:T(8,128)S(1)} collective-permute-done((f32[8,128]{1,0:T(8,128)S(1)}, f32[8,128]{1,0:T(8,128)S(1)}, u32[]{:S(2)}, u32[]{:S(2)}) %collective-permute-start.11) | collective-permute-done | bytes 4128 | tf_op jit(solution)/shard_map/ppermute | solution.py:16
  60.2 0.6 collective-permute-start.23
  60.9 6.5 %collective-permute-done.12 = f32[8,128]{1,0:T(8,128)S(1)} collective-permute-done((f32[8,128]{1,0:T(8,128)S(1)}, f32[8,128]{1,0:T(8,128)S(1)}, u32[]{:S(2)}, u32[]{:S(2)}) %collective-permute-start.12) | collective-permute-done | bytes 4128 | tf_op jit(solution)/shard_map/ppermute | solution.py:16
  67.4 0.5 collective-permute-start.20
  67.9 3.5 %collective-permute-start.13 = (f32[8,128]{1,0:T(8,128)S(1)}, f32[8,128]{1,0:T(8,128)S(1)}, u32[]{:S(2)}, u32[]{:S(2)}) collective-permute-start(f32[8,128]{1,0:T(8,128)S(1)} %add.43.refs_0_), channel_id=1, source_target_pairs={{0,12},{1,13},{2,14},{3,15},{4,8},{5,9},{6,10},{7,11},{8,4},{9,5},... | collective-permute-start | bytes 12296 | tf_op jit(solution)/shard_map/ppermute | solution.py:16
  71.6 1.6 %collective-permute-start.22 = (bf16[128,1024]{1,0:T(8,128)(2,1)S(1)}, bf16[128,1024]{1,0:T(8,128)(2,1)S(1)}, u32[]{:S(2)}, u32[]{:S(2)}) collective-permute-start(bf16[128,1024]{1,0:T(8,128)(2,1)S(1)} %shard_map.78), channel_id=1, source_target_pairs={{0,2},{1,3},{2,0},{3,1},{4,6},{5,7},{6,4},{7,5},{8,10},{9,11},{10,... | collective-permute-start | bytes 786440 | tf_op jit(solution)/shard_map/ppermute | solution.py:16
  73.1 0.1 shard_map.80
  73.2 3.3 %collective-permute-done.20.refs_2_ = bf16[128,1024]{1,0:T(8,128)(2,1)S(1)} collective-permute-done((bf16[128,1024]{1,0:T(8,128)(2,1)S(1)}, bf16[128,1024]{1,0:T(8,128)(2,1)S(1)}, u32[]{:S(2)}, u32[]{:S(2)}) %collective-permute-start.20) | collective-permute-done | bytes 262176 | tf_op jit(solution)/shard_map/ppermute | solution.py:16
  76.6 2.5 %collective-permute-start.24 = (bf16[128,1024]{1,0:T(8,128)(2,1)S(1)}, bf16[128,1024]{1,0:T(8,128)(2,1)S(1)}, u32[]{:S(2)}, u32[]{:S(2)}) collective-permute-start(bf16[128,1024]{1,0:T(8,128)(2,1)S(1)} %shard_map.80), channel_id=1, source_target_pairs={{0,4},{1,5},{2,6},{3,7},{4,0},{5,1},{6,2},{7,3},{8,12},{9,13},{10,... | collective-permute-start | bytes 786440 | tf_op jit(solution)/shard_map/ppermute | solution.py:16
  79.0 0.1 shard_map.77
  79.1 0.6 collective-permute-start.17
  79.7 1.6 %shard_map.73 = (f32[1]{0:T(128)}, f32[256,1,1024]{2,1,0:T(1,128)}) custom-call(f32[8,128]{1,0:T(8,128)S(1)} %add.43.refs_0_, f32[8,128]{1,0:T(8,128)S(1)} %collective-permute-done.13.refs_1_, f32[256,1024]{1,0:T(8,128)S(1)} %get-tuple-element.46.refs_2_, bf16[256,1024]{1,0:T(8,128)(2,1)S(1)} %collective-permute-done.14.refs_3_), custom_call_target="tpu_custom_call" | custom-call | flops 1048576 | bytes 3670016 | tf_op jit(solution)/shard_map/pallas_call | solution.py:237
  81.3 0.9 collective-permute-done.22.refs_2_
  82.2 4.0 %collective-permute-done.24.refs_3_ = bf16[128,1024]{1,0:T(8,128)(2,1)S(1)} collective-permute-done((bf16[128,1024]{1,0:T(8,128)(2,1)S(1)}, bf16[128,1024]{1,0:T(8,128)(2,1)S(1)}, u32[]{:S(2)}, u32[]{:S(2)}) %collective-permute-start.24) | collective-permute-done | bytes 262176 | tf_op jit(solution)/shard_map/ppermute | solution.py:16
  86.2 0.8 shard_map.81.refs_4_
  87.1 0.3 collective-permute-done.17.refs_2_
  87.3 3.0 %collective-permute-done.21.refs_3_ = bf16[128,1024]{1,0:T(8,128)(2,1)S(1)} collective-permute-done((bf16[128,1024]{1,0:T(8,128)(2,1)S(1)}, bf16[128,1024]{1,0:T(8,128)(2,1)S(1)}, u32[]{:S(2)}, u32[]{:S(2)}) %collective-permute-start.21) | collective-permute-done | bytes 262176 | tf_op jit(solution)/shard_map/ppermute | solution.py:16
  90.3 0.9 shard_map.82
  (31 shorter events, 0.4 us)
Async XLA Ops:
  0.6 15.3 %collective-permute-start.1 = (bf16[256,1024]{1,0:T(8,128)(2,1)}, bf16[256,1024]{1,0:T(8,128)(2,1)S(1)}, u32[]{:S(2)}, u32[]{:S(2)}) collective-permute-start(bf16[256,1024]{1,0:T(8,128)(2,1)} %bitcast.6), channel_id=1, source_target_pairs={{0,4},{1,5},{2,6},{3,7},{4,0},{5,1},{6,2},{7,3},{8,12},{9,13},{10,... | collective-permute-start | bytes 1572872 | tf_op jit(solution)/shard_map/ppermute | solution.py:16
  3.7 19.3 %collective-permute-start.3 = (bf16[256,1024]{1,0:T(8,128)(2,1)}, bf16[256,1024]{1,0:T(8,128)(2,1)S(1)}, u32[]{:S(2)}, u32[]{:S(2)}) collective-permute-start(bf16[256,1024]{1,0:T(8,128)(2,1)} %bitcast.7), channel_id=1, source_target_pairs={{0,2},{1,3},{2,0},{3,1},{4,6},{5,7},{6,4},{7,5},{8,10},{9,11},{10,... | collective-permute-start | bytes 1572872 | tf_op jit(solution)/shard_map/ppermute | solution.py:16
  5.3 18.1 %collective-permute-start.6 = (bf16[256,1024]{1,0:T(8,128)(2,1)}, bf16[256,1024]{1,0:T(8,128)(2,1)S(1)}, u32[]{:S(2)}, u32[]{:S(2)}) collective-permute-start(bf16[256,1024]{1,0:T(8,128)(2,1)} %bitcast.10), channel_id=1, source_target_pairs={{4,8},{5,9},{6,10},{7,11},{8,4},{9,5},{10,6},{11,7},{20,24},{21,25... | collective-permute-start | bytes 1572872 | tf_op jit(solution)/shard_map/ppermute | solution.py:16
  15.9 13.1 %collective-permute-start.8 = (bf16[256,1024]{1,0:T(8,128)(2,1)S(1)}, bf16[256,1024]{1,0:T(8,128)(2,1)S(1)}, u32[]{:S(2)}, u32[]{:S(2)}) collective-permute-start(bf16[256,1024]{1,0:T(8,128)(2,1)S(1)} %collective-permute-done.1.refs_1_), channel_id=1, source_target_pairs={{0,2},{1,3},{2,0},{3,1},{4,6},{5,7},{6,4},{7,5},{8,10},{9,11},{10,... | collective-permute-start | bytes 1572872 | tf_op jit(solution)/shard_map/ppermute | solution.py:16
  17.6 22.0 %collective-permute-start = (bf16[256,1024]{1,0:T(8,128)(2,1)}, bf16[256,1024]{1,0:T(8,128)(2,1)S(1)}, u32[]{:S(2)}, u32[]{:S(2)}) collective-permute-start(bf16[256,1024]{1,0:T(8,128)(2,1)} %bitcast.8), channel_id=1, source_target_pairs={{0,1},{1,0},{2,3},{3,2},{4,5},{5,4},{6,7},{7,6},{8,9},{9,8},{10,11... | collective-permute-start | bytes 1572872 | tf_op jit(solution)/shard_map/ppermute | solution.py:16
  17.6 18.3 %collective-permute-start.7 = (bf16[256,1024]{1,0:T(8,128)(2,1)}, bf16[256,1024]{1,0:T(8,128)(2,1)S(1)}, u32[]{:S(2)}, u32[]{:S(2)}) collective-permute-start(bf16[256,1024]{1,0:T(8,128)(2,1)} %bitcast.11), channel_id=1, source_target_pairs={{0,12},{1,13},{2,14},{3,15},{12,0},{13,1},{14,2},{15,3},{16,28},{1... | collective-permute-start | bytes 1572872 | tf_op jit(solution)/shard_map/ppermute | solution.py:16
  23.1 20.0 %collective-permute-start.2 = (bf16[256,1024]{1,0:T(8,128)(2,1)S(1)}, bf16[256,1024]{1,0:T(8,128)(2,1)S(1)}, u32[]{:S(2)}, u32[]{:S(2)}) collective-permute-start(bf16[256,1024]{1,0:T(8,128)(2,1)S(1)} %collective-permute-done.1.refs_1_), channel_id=1, source_target_pairs={{0,1},{1,0},{2,3},{3,2},{4,5},{5,4},{6,7},{7,6},{8,9},{9,8},{10,11... | collective-permute-start | bytes 1572872 | tf_op jit(solution)/shard_map/ppermute | solution.py:16
  23.4 19.8 %collective-permute-start.4 = (bf16[256,1024]{1,0:T(8,128)(2,1)S(1)}, bf16[256,1024]{1,0:T(8,128)(2,1)S(1)}, u32[]{:S(2)}, u32[]{:S(2)}) collective-permute-start(bf16[256,1024]{1,0:T(8,128)(2,1)S(1)} %collective-permute-done.3.refs_3_), channel_id=1, source_target_pairs={{0,1},{1,0},{2,3},{3,2},{4,5},{5,4},{6,7},{7,6},{8,9},{9,8},{10,11... | collective-permute-start | bytes 1572872 | tf_op jit(solution)/shard_map/ppermute | solution.py:16
  29.0 18.3 %collective-permute-start.9 = (bf16[256,1024]{1,0:T(8,128)(2,1)S(1)}, bf16[256,1024]{1,0:T(8,128)(2,1)S(1)}, u32[]{:S(2)}, u32[]{:S(2)}) collective-permute-start(bf16[256,1024]{1,0:T(8,128)(2,1)S(1)} %collective-permute-done.8.refs_2_), channel_id=1, source_target_pairs={{0,1},{1,0},{2,3},{3,2},{4,5},{5,4},{6,7},{7,6},{8,9},{9,8},{10,11... | collective-permute-start | bytes 1572872 | tf_op jit(solution)/shard_map/ppermute | solution.py:16
  35.9 9.2 %collective-permute-start.5 = (f32[32]{0:T(128)S(1)}, f32[32]{0:T(128)S(1)}, u32[]{:S(2)}, u32[]{:S(2)}) collective-permute-start(f32[32]{0:T(128)S(1)} %pad_maximum_fusion.refs_0_), channel_id=1, source_target_pairs={{0,12},{1,13},{2,14},{3,15},{4,8},{5,9},{6,10},{7,11},{8,4},{9,5},... | collective-permute-start | bytes 392 | tf_op jit(solution)/shard_map/ppermute | solution.py:16
  39.6 1.0 %copy-start = (bf16[256,1,1024]{2,0,1:T(8,128)(2,1)S(1)}, bf16[256,1,1024]{2,0,1:T(8,128)(2,1)}, u32[]{:S(2)}) copy-start(bf16[256,1,1024]{2,0,1:T(8,128)(2,1)} %param.5) | copy-start | bytes 1572868
  40.7 1.0 %copy-start.1 = (bf16[256,1,1024]{2,0,1:T(8,128)(2,1)S(1)}, bf16[256,1,1024]{2,0,1:T(8,128)(2,1)}, u32[]{:S(2)}) copy-start(bf16[256,1,1024]{2,0,1:T(8,128)(2,1)} %param.4) | copy-start | bytes 1572868
  49.9 10.3 %collective-permute-start.19 = (bf16[256,1024]{1,0:T(8,128)(2,1)S(1)}, bf16[256,1024]{1,0:T(8,128)(2,1)S(1)}, u32[]{:S(2)}, u32[]{:S(2)}) collective-permute-start(bf16[256,1024]{1,0:T(8,128)(2,1)S(1)} %get-tuple-element.56), channel_id=1, source_target_pairs={{0,1},{1,0},{2,3},{3,2},{4,5},{5,4},{6,7},{7,6},{8,9},{9,8},{10,11... | collective-permute-start | bytes 1572872 | tf_op jit(solution)/shard_map/ppermute | solution.py:16
  52.3 15.0 %collective-permute-start.18 = (bf16[256,1024]{1,0:T(8,128)(2,1)S(1)}, bf16[256,1024]{1,0:T(8,128)(2,1)S(1)}, u32[]{:S(2)}, u32[]{:S(2)}) collective-permute-start(bf16[256,1024]{1,0:T(8,128)(2,1)S(1)} %get-tuple-element.54), channel_id=1, source_target_pairs={{0,1},{1,0},{2,3},{3,2},{4,5},{5,4},{6,7},{7,6},{8,9},{9,8},{10,11... | collective-permute-start | bytes 1572872 | tf_op jit(solution)/shard_map/ppermute | solution.py:16
  53.6 14.3 %collective-permute-start.16 = (bf16[256,1024]{1,0:T(8,128)(2,1)S(1)}, bf16[256,1024]{1,0:T(8,128)(2,1)S(1)}, u32[]{:S(2)}, u32[]{:S(2)}) collective-permute-start(bf16[256,1024]{1,0:T(8,128)(2,1)S(1)} %get-tuple-element.52), channel_id=1, source_target_pairs={{0,1},{1,0},{2,3},{3,2},{4,5},{5,4},{6,7},{7,6},{8,9},{9,8},{10,11... | collective-permute-start | bytes 1572872 | tf_op jit(solution)/shard_map/ppermute | solution.py:16
  55.0 24.7 %collective-permute-start.14 = (bf16[256,1024]{1,0:T(8,128)(2,1)S(1)}, bf16[256,1024]{1,0:T(8,128)(2,1)S(1)}, u32[]{:S(2)}, u32[]{:S(2)}) collective-permute-start(bf16[256,1024]{1,0:T(8,128)(2,1)S(1)} %shard_map.72), channel_id=1, source_target_pairs={{0,12},{1,13},{2,14},{3,15},{4,8},{5,9},{6,10},{7,11},{8,4},{9,5},... | collective-permute-start | bytes 1572872 | tf_op jit(solution)/shard_map/ppermute | solution.py:16
  55.4 1.2 %collective-permute-start.10 = (f32[8,128]{1,0:T(8,128)S(1)}, f32[8,128]{1,0:T(8,128)S(1)}, u32[]{:S(2)}, u32[]{:S(2)}) collective-permute-start(f32[8,128]{1,0:T(8,128)S(1)} %add_add_fusion), channel_id=1, source_target_pairs={{0,1},{1,0},{2,3},{3,2},{4,5},{5,4},{6,7},{7,6},{8,9},{9,8},{10,11... | collective-permute-start | bytes 12296 | tf_op jit(solution)/shard_map/ppermute | solution.py:16
  56.5 3.6 %collective-permute-start.11 = (f32[8,128]{1,0:T(8,128)S(1)}, f32[8,128]{1,0:T(8,128)S(1)}, u32[]{:S(2)}, u32[]{:S(2)}) collective-permute-start(f32[8,128]{1,0:T(8,128)S(1)} %add.41), channel_id=1, source_target_pairs={{0,2},{1,3},{2,0},{3,1},{4,6},{5,7},{6,4},{7,5},{8,10},{9,11},{10,... | collective-permute-start | bytes 12296 | tf_op jit(solution)/shard_map/ppermute | solution.py:16
  60.2 7.2 %collective-permute-start.12 = (f32[8,128]{1,0:T(8,128)S(1)}, f32[8,128]{1,0:T(8,128)S(1)}, u32[]{:S(2)}, u32[]{:S(2)}) collective-permute-start(f32[8,128]{1,0:T(8,128)S(1)} %add.42), channel_id=1, source_target_pairs={{0,4},{1,5},{2,6},{3,7},{4,0},{5,1},{6,2},{7,3},{8,12},{9,13},{10,... | collective-permute-start | bytes 12296 | tf_op jit(solution)/shard_map/ppermute | solution.py:16
  60.2 11.3 %collective-permute-start.23 = (bf16[128,1024]{1,0:T(8,128)(2,1)S(1)}, bf16[128,1024]{1,0:T(8,128)(2,1)S(1)}, u32[]{:S(2)}, u32[]{:S(2)}) collective-permute-start(bf16[128,1024]{1,0:T(8,128)(2,1)S(1)} %shard_map.79), channel_id=1, source_target_pairs={{0,2},{1,3},{2,0},{3,1},{4,6},{5,7},{6,4},{7,5},{8,10},{9,11},{10,... | collective-permute-start | bytes 786440 | tf_op jit(solution)/shard_map/ppermute | solution.py:16
  67.4 13.9 %collective-permute-start.15 = (bf16[256,1024]{1,0:T(8,128)(2,1)S(1)}, bf16[256,1024]{1,0:T(8,128)(2,1)S(1)}, u32[]{:S(2)}, u32[]{:S(2)}) collective-permute-start(bf16[256,1024]{1,0:T(8,128)(2,1)S(1)} %get-tuple-element.50), channel_id=1, source_target_pairs={{0,1},{1,0},{2,3},{3,2},{4,5},{5,4},{6,7},{7,6},{8,9},{9,8},{10,11... | collective-permute-start | bytes 1572872 | tf_op jit(solution)/shard_map/ppermute | solution.py:16
  67.4 9.2 %collective-permute-start.20 = (bf16[128,1024]{1,0:T(8,128)(2,1)S(1)}, bf16[128,1024]{1,0:T(8,128)(2,1)S(1)}, u32[]{:S(2)}, u32[]{:S(2)}) collective-permute-start(bf16[128,1024]{1,0:T(8,128)(2,1)S(1)} %shard_map.76), channel_id=1, source_target_pairs={{0,2},{1,3},{2,0},{3,1},{4,6},{5,7},{6,4},{7,5},{8,10},{9,11},{10,... | collective-permute-start | bytes 786440 | tf_op jit(solution)/shard_map/ppermute | solution.py:16
  67.9 11.2 %collective-permute-start.13 = (f32[8,128]{1,0:T(8,128)S(1)}, f32[8,128]{1,0:T(8,128)S(1)}, u32[]{:S(2)}, u32[]{:S(2)}) collective-permute-start(f32[8,128]{1,0:T(8,128)S(1)} %add.43.refs_0_), channel_id=1, source_target_pairs={{0,12},{1,13},{2,14},{3,15},{4,8},{5,9},{6,10},{7,11},{8,4},{9,5},... | collective-permute-start | bytes 12296 | tf_op jit(solution)/shard_map/ppermute | solution.py:16
  71.6 10.6 %collective-permute-start.22 = (bf16[128,1024]{1,0:T(8,128)(2,1)S(1)}, bf16[128,1024]{1,0:T(8,128)(2,1)S(1)}, u32[]{:S(2)}, u32[]{:S(2)}) collective-permute-start(bf16[128,1024]{1,0:T(8,128)(2,1)S(1)} %shard_map.78), channel_id=1, source_target_pairs={{0,2},{1,3},{2,0},{3,1},{4,6},{5,7},{6,4},{7,5},{8,10},{9,11},{10,... | collective-permute-start | bytes 786440 | tf_op jit(solution)/shard_map/ppermute | solution.py:16
  76.6 9.6 %collective-permute-start.24 = (bf16[128,1024]{1,0:T(8,128)(2,1)S(1)}, bf16[128,1024]{1,0:T(8,128)(2,1)S(1)}, u32[]{:S(2)}, u32[]{:S(2)}) collective-permute-start(bf16[128,1024]{1,0:T(8,128)(2,1)S(1)} %shard_map.80), channel_id=1, source_target_pairs={{0,4},{1,5},{2,6},{3,7},{4,0},{5,1},{6,2},{7,3},{8,12},{9,13},{10,... | collective-permute-start | bytes 786440 | tf_op jit(solution)/shard_map/ppermute | solution.py:16
  79.1 8.2 %collective-permute-start.17 = (bf16[128,1024]{1,0:T(8,128)(2,1)S(1)}, bf16[128,1024]{1,0:T(8,128)(2,1)S(1)}, u32[]{:S(2)}, u32[]{:S(2)}) collective-permute-start(bf16[128,1024]{1,0:T(8,128)(2,1)S(1)} %shard_map.75), channel_id=1, source_target_pairs={{0,2},{1,3},{2,0},{3,1},{4,6},{5,7},{6,4},{7,5},{8,10},{9,11},{10,... | collective-permute-start | bytes 786440 | tf_op jit(solution)/shard_map/ppermute | solution.py:16
  79.7 10.6 %collective-permute-start.21 = (bf16[128,1024]{1,0:T(8,128)(2,1)S(1)}, bf16[128,1024]{1,0:T(8,128)(2,1)S(1)}, u32[]{:S(2)}, u32[]{:S(2)}) collective-permute-start(bf16[128,1024]{1,0:T(8,128)(2,1)S(1)} %shard_map.77), channel_id=1, source_target_pairs={{0,4},{1,5},{2,6},{3,7},{4,0},{5,1},{6,2},{7,3},{8,12},{9,13},{10,... | collective-permute-start | bytes 786440 | tf_op jit(solution)/shard_map/ppermute | solution.py:16
